TPU v7x, 128 devices: a whole 4x4x4 slice. The times are simulated.
128 devices in a mesh: row: 16 (over y, z), col: 8 (over x, core).
Axes of the slice: x: 4, y: 4, z: 4, core: 2. Of those that a mesh axis runs over, the one named last changes fastest.
Arguments:
- tokens: bfloat16 [2048, 4096], P('row', 'col'), may hold values from -6 to 6
- w_in: bfloat16 [4096, 16384], P('col', 'row'), may hold values from -0.09375 to 0.09375
- w_out: bfloat16 [16384, 4096], P('row', 'col'), may hold values from -0.046875 to 0.046875
- cotangent: bfloat16 [2048, 4096], P('row', 'col'), may hold values from -6 to 6
Outputs:
- block_out: bfloat16 [2048, 4096], P(('row', 'col'))
- grad_tokens: bfloat16 [2048, 4096], P('row', 'col')
- grad_in: float32 [4096, 16384], P('col', 'row')
- grad_out: float32 [16384, 4096], P('row', 'col')
All inputs are finite; a program needn't handle non-finite values.
Results may differ from a plain program's by a relative error of at most 0.015.
Values may be sent and summed in bfloat16 or wider, within the bound.
A program may use at most 128 MiB of HBM per device.

v0:
```python
import jax
import jax.numpy as jnp
from jax import lax
from jax.sharding import PartitionSpec as P


def gelu_grad(value):
    cdf = 0.5 * (1.0 + jax.scipy.special.erf(value * 0.7071067811865476))
    pdf = jnp.exp(-0.5 * value * value) * 0.3989422804014327
    return cdf + value * pdf


def token_panel(local_rows):
    return lax.all_gather(local_rows, "row", axis=0, tiled=True)


def token_panel_a2a(local_rows):
    n = lax.axis_size("row")
    copies = jnp.broadcast_to(local_rows[None], (n,) + local_rows.shape)
    copies = copies.reshape(n * local_rows.shape[0], local_rows.shape[1])
    return lax.all_to_all(copies, "row", split_axis=0, concat_axis=0, tiled=True)


def hidden_panel(local_rows):
    return lax.all_gather(local_rows, "col", axis=0, tiled=True)


def contract_last(left, right):
    return lax.dot_general(
        left, right, (((1,), (1,)), ((), ())), preferred_element_type=jnp.float32
    )


def width_split(left_all, right, transposed):
    if transposed:
        term = contract_last(left_all, right)
    else:
        term = jnp.dot(left_all, right, preferred_element_type=jnp.float32)
    return lax.psum_scatter(
        term.astype(jnp.bfloat16), "col", scatter_dimension=0, tiled=True
    ).astype(jnp.float32)


def unit_sum(left_all, right, transposed):
    n = lax.axis_size("row")
    if transposed:
        term = contract_last(left_all, right)
    else:
        term = jnp.dot(left_all, right, preferred_element_type=jnp.float32)
    pieces = term.astype(jnp.bfloat16).reshape(n, term.shape[0] // n, term.shape[1])
    pieces = lax.all_to_all(pieces, "row", split_axis=0, concat_axis=0, tiled=True)
    return jnp.sum(pieces.astype(jnp.float32), axis=0)


def local(tokens, w_in, w_out, cotangent):
    tokens_all = token_panel(tokens)
    upstream_all = token_panel_a2a(cotangent)
    pre_part = width_split(tokens_all, w_in, False)
    act_all = hidden_panel(jax.nn.gelu(pre_part, approximate=False).astype(jnp.bfloat16))
    dact_part = width_split(upstream_all, w_out, True)
    dpre_all = hidden_panel((dact_part * gelu_grad(pre_part)).astype(jnp.bfloat16))
    mixed = unit_sum(act_all, w_out, False)
    block_rows = (tokens.astype(jnp.float32) + mixed).astype(jnp.bfloat16)
    block_out = lax.all_to_all(block_rows, "col", split_axis=0, concat_axis=1, tiled=True)
    grad_out = lax.dot_general(
        act_all, upstream_all, (((0,), (0,)), ((), ())), preferred_element_type=jnp.float32
    )
    grad_in = lax.dot_general(
        tokens_all, dpre_all, (((0,), (0,)), ((), ())), preferred_element_type=jnp.float32
    )
    back = unit_sum(dpre_all, w_in, True)
    grad_tokens = (cotangent.astype(jnp.float32) + back).astype(jnp.bfloat16)
    return (block_out, grad_tokens, grad_in, grad_out)


def solution(mesh):
    in_specs = (P("row", "col"), P("col", "row"), P("row", "col"), P("row", "col"))
    out_specs = (P(("row", "col"), None), P("row", "col"), P("col", "row"), P("row", "col"))
    return jax.shard_map(local, mesh=mesh, in_specs=in_specs, out_specs=out_specs, check_vma=False)
```

profile of v0, /device:TPU:1, one launch (start us, length us, event | category | flops | bytes accessed | tf_op | source)
XLA Modules:
  0.0 260.2 jit_solution(16874489885100301524)
XLA Ops:
  8.8 1.1 broadcast_in_dim.2
  9.9 37.6 %all_to_all.38 = bf16[16,128,512]{2,1,0:T(8,128)(2,1)S(1)} all-to-all(bf16[16,128,512]{2,1,0:T(8,128)(2,1)S(1)} %broadcast_in_dim.2), channel_id=1, replica_groups=mesh['row'=16,'col'=8] {'row'}, dimensions={0} | all-to-all | bytes 4194304 | tf_op jit(solution)/shard_map/all_to_all | solution.py:21
  47.5 1.4 copy-done.1
  48.9 4.3 %convolution_convert_fusion = bf16[2048,1024]{1,0:T(8,128)(2,1)} fusion(bf16[2048,512]{1,0:T(8,128)(2,1)S(1)} %bitcast.21, bf16[1024,512]{1,0:T(8,128)(2,1)S(1)} %copy-done), kind=kOutput, calls=%fused_computation.2 | convolution fusion | flops 2149580800 | bytes 7340032 | tf_op jit(solution)/shard_map/dot_general | solution.py:29
  53.3 12.5 %all-gather.4.cloned.1.call-done = bf16[2048,512]{1,0:T(8,128)(2,1)} async-done(((bf16[128,512]{1,0:T(8,128)(2,1)}), bf16[2048,512]{1,0:T(8,128)(2,1)}) %all-gather.4.cloned.1.call-update) | async-done | bytes 2097168 | tf_op jit(solution)/shard_map/all_gather | solution.py:14
  65.8 5.9 %convolution_convert_fusion.1 = bf16[2048,1024]{1,0:T(8,128)(2,1)} fusion(bf16[2048,512]{1,0:T(8,128)(2,1)} %all-gather.4.cloned.1.call-done, bf16[512,1024]{1,0:T(8,128)(2,1)S(1)} %copy-done.4), kind=kOutput, calls=%fused_computation.3 | convolution fusion | flops 2149580800 | bytes 7340032 | tf_op jit(solution)/shard_map/dot_general | solution.py:38
  71.9 15.8 %reduce-scatter.5.cloned.1.call-done = bf16[256,1024]{1,0:T(8,128)(2,1)} async-done(((bf16[2048,1024]{1,0:T(8,128)(2,1)}), bf16[256,1024]{1,0:T(8,128)(2,1)}) %reduce-scatter.5.cloned.1.call-update) | async-done | bytes 524304 | tf_op jit(solution)/shard_map/reduce_scatter | solution.py:39
  87.7 38.8 %reduce-scatter.3.cloned.1.call-done = bf16[256,1024]{1,0:T(8,128)(2,1)} async-done(((bf16[2048,1024]{1,0:T(8,128)(2,1)}), bf16[256,1024]{1,0:T(8,128)(2,1)}) %reduce-scatter.3.cloned.1.call-update) | async-done | bytes 524304 | tf_op jit(solution)/shard_map/reduce_scatter | solution.py:39
  126.4 4.6 %fusion.38 = (bf16[256,1024]{1,0:T(8,128)(2,1)}, bf16[256,1024]{1,0:T(8,128)(2,1)}) fusion(bf16[256,1024]{1,0:T(8,128)(2,1)} %reduce-scatter.3.cloned.1.call-done, bf16[256,1024]{1,0:T(8,128)(2,1)} %reduce-scatter.5.cloned.1.call-done), kind=kLoop, calls=%fused_computation.52 | loop fusion | flops 20185088 | bytes 2097152 | tf_op jit(solution)/shard_map/convert_element_type | solution.py:61
  131.8 33.5 %all-gather.6.cloned.1.call-done = bf16[2048,1024]{1,0:T(8,128)(2,1)} async-done(((bf16[256,1024]{1,0:T(8,128)(2,1)}), bf16[2048,1024]{1,0:T(8,128)(2,1)}) %all-gather.6.cloned.1.call-update) | async-done | bytes 4194320 | tf_op jit(solution)/shard_map/all_gather | solution.py:25
  165.3 5.8 %convolution_convert_fusion.3 = bf16[2048,512]{1,0:T(8,128)(2,1)} fusion(bf16[2048,1024]{1,0:T(8,128)(2,1)} %all-gather.6.cloned.1.call-done, bf16[1024,512]{1,0:T(8,128)(2,1)S(1)} %copy-done), kind=kOutput, calls=%fused_computation.5 | convolution fusion | flops 2148532224 | bytes 7340032 | tf_op jit(solution)/shard_map/dot_general | solution.py:49
  171.1 6.7 %all-to-all-start = ((bf16[16,128,512]{2,1,0:T(8,128)(2,1)}), bf16[16,128,512]{2,1,0:T(8,128)(2,1)S(1)}, u32[]{:S(2)}, u32[]{:S(2)}) async-start(bf16[16,128,512]{2,1,0:T(8,128)(2,1)} %bitcast.24), calls=%async_computation.1 | async-start | bytes 4194304 | tf_op jit(solution)/shard_map/all_to_all | solution.py:51
  177.9 21.7 %all-gather.8.cloned.1.call-done = bf16[2048,1024]{1,0:T(8,128)(2,1)} async-done(((bf16[256,1024]{1,0:T(8,128)(2,1)}), bf16[2048,1024]{1,0:T(8,128)(2,1)}) %all-gather.8.cloned.1.call-update) | async-done | bytes 4194320 | tf_op jit(solution)/shard_map/all_gather | solution.py:25
  199.5 6.2 %convolution_convert_fusion.2 = bf16[2048,512]{1,0:T(8,128)(2,1)} fusion(bf16[2048,1024]{1,0:T(8,128)(2,1)} %all-gather.8.cloned.1.call-done, bf16[512,1024]{1,0:T(8,128)(2,1)} %param.5), kind=kOutput, calls=%fused_computation.4 | convolution fusion | flops 2148532224 | bytes 7340032 | tf_op jit(solution)/shard_map/dot_general | solution.py:29
  205.7 1.4 all-to-all-done
  207.1 5.4 %all-to-all-start.3 = ((bf16[16,128,512]{2,1,0:T(8,128)(2,1)}), bf16[16,128,512]{2,1,0:T(8,128)(2,1)}, u32[]{:S(2)}, u32[]{:S(2)}) async-start(bf16[16,128,512]{2,1,0:T(8,128)(2,1)} %bitcast.23), calls=%async_computation.5 | async-start | bytes 4194304 | tf_op jit(solution)/shard_map/all_to_all | solution.py:51
  212.5 6.6 %convolution_bitcast_fusion = f32[512,1024]{0,1:T(8,128)} fusion(bf16[2048,1024]{1,0:T(8,128)(2,1)} %all-gather.8.cloned.1.call-done, bf16[2048,512]{1,0:T(8,128)(2,1)} %all-gather.4.cloned.1.call-done), kind=kOutput, calls=%fused_computation.12 | convolution fusion | flops 2147483648 | bytes 8388608 | tf_op jit(solution)/shard_map/dot_general | solution.py:68
  219.0 2.9 %copy.12 = f32[512,1024]{1,0:T(8,128)} copy(f32[512,1024]{0,1:T(8,128)} %convolution_bitcast_fusion) | data formatting | bytes 4194304
  221.9 6.5 %fusion.39 = f32[1024,512]{1,0:T(8,128)} fusion(bf16[2048,1024]{1,0:T(8,128)(2,1)} %all-gather.6.cloned.1.call-done, bf16[2048,512]{1,0:T(8,128)(2,1)} %bitcast.22), kind=kOutput, calls=%fused_computation.55 | convolution fusion | flops 2147483648 | bytes 8388608 | tf_op jit(solution)/shard_map/dot_general | solution.py:65
  230.0 8.0 %all-to-all-done.3 = bf16[16,128,512]{2,1,0:T(8,128)(2,1)} async-done(((bf16[16,128,512]{2,1,0:T(8,128)(2,1)}), bf16[16,128,512]{2,1,0:T(8,128)(2,1)}, u32[]{:S(2)}, u32[]{:S(2)}) %all-to-all-start.3) | async-done | bytes 2097184 | tf_op jit(solution)/shard_map/all_to_all | solution.py:51
  238.1 8.6 %all-to-all-start.1 = ((bf16[8,16,512]{2,1,0:T(8,128)(2,1)}), bf16[8,16,512]{2,1,0:T(8,128)(2,1)S(1)}, u32[]{:S(2)}, u32[]{:S(2)}) async-start(bf16[8,16,512]{2,1,0:T(8,128)(2,1)} %bitcast.1), calls=%async_computation.2 | async-start | bytes 262144 | tf_op jit(solution)/shard_map/all_to_all | solution.py:64
  246.7 1.9 convert_reduce_fusion
  248.6 0.7 add_convert_fusion
  249.3 2.7 %all-to-all-done.1 = bf16[8,16,512]{2,1,0:T(8,128)(2,1)S(1)} async-done(((bf16[8,16,512]{2,1,0:T(8,128)(2,1)}), bf16[8,16,512]{2,1,0:T(8,128)(2,1)S(1)}, u32[]{:S(2)}, u32[]{:S(2)}) %all-to-all-start.1) | async-done | bytes 131104 | tf_op jit(solution)/shard_map/all_to_all | solution.py:64
  (22 shorter events, 3.9 us)
Async XLA Ops:
  8.0 40.9 %copy-start = (bf16[1024,512]{1,0:T(8,128)(2,1)S(1)}, bf16[1024,512]{1,0:T(8,128)(2,1)}, u32[]{:S(2)}) copy-start(bf16[1024,512]{1,0:T(8,128)(2,1)} %param.6) | copy-start | bytes 3145732
  8.0 57.8 %all-gather.4.cloned.1.call-start = ((), (), s32[]{:S(2)}) async-start(), calls=%async_computation.6 | async-start | bytes 2228224 | tf_op jit(solution)/shard_map/all_gather | solution.py:14
  8.7 78.9 %reduce-scatter.5.cloned.1.call-start = ((), (), s32[]{:S(2)}) async-start(), calls=%async_computation.9 | async-start | bytes 4718592 | tf_op jit(solution)/shard_map/reduce_scatter | solution.py:39
  47.5 1.4 copy-start.1
  53.2 12.6 %copy-start.4 = (bf16[512,1024]{1,0:T(8,128)(2,1)S(1)}, bf16[512,1024]{1,0:T(8,128)(2,1)}, u32[]{:S(2)}) copy-start(bf16[512,1024]{1,0:T(8,128)(2,1)} %param.5) | copy-start | bytes 3145732
  53.3 73.2 %reduce-scatter.3.cloned.1.call-start = ((), (), s32[]{:S(2)}) async-start(), calls=%async_computation.7 | async-start | bytes 4718592 | tf_op jit(solution)/shard_map/reduce_scatter | solution.py:39
  71.8 93.5 %all-gather.6.cloned.1.call-start = ((), (), s32[]{:S(2)}) async-start(), calls=%async_computation.8 | async-start | bytes 4718592 | tf_op jit(solution)/shard_map/all_gather | solution.py:25
  131.0 68.5 %all-gather.8.cloned.1.call-start = ((), (), s32[]{:S(2)}) async-start(), calls=%async_computation.10 | async-start | bytes 4718592 | tf_op jit(solution)/shard_map/all_gather | solution.py:25
  171.1 35.9 %all-to-all-start = ((bf16[16,128,512]{2,1,0:T(8,128)(2,1)}), bf16[16,128,512]{2,1,0:T(8,128)(2,1)S(1)}, u32[]{:S(2)}, u32[]{:S(2)}) async-start(bf16[16,128,512]{2,1,0:T(8,128)(2,1)} %bitcast.24), calls=%async_computation.1 | async-start | bytes 4194304 | tf_op jit(solution)/shard_map/all_to_all | solution.py:51
  207.1 31.0 %all-to-all-start.3 = ((bf16[16,128,512]{2,1,0:T(8,128)(2,1)}), bf16[16,128,512]{2,1,0:T(8,128)(2,1)}, u32[]{:S(2)}, u32[]{:S(2)}) async-start(bf16[16,128,512]{2,1,0:T(8,128)(2,1)} %bitcast.23), calls=%async_computation.5 | async-start | bytes 4194304 | tf_op jit(solution)/shard_map/all_to_all | solution.py:51
  228.5 0.9 copy-start.3
  229.4 19.2 %copy-start.2 = (bf16[128,512]{1,0:T(8,128)(2,1)S(1)}, bf16[128,512]{1,0:T(8,128)(2,1)}, u32[]{:S(2)}) copy-start(bf16[128,512]{1,0:T(8,128)(2,1)} %param.7) | copy-start | bytes 393220
  238.1 13.9 %all-to-all-start.1 = ((bf16[8,16,512]{2,1,0:T(8,128)(2,1)}), bf16[8,16,512]{2,1,0:T(8,128)(2,1)S(1)}, u32[]{:S(2)}, u32[]{:S(2)}) async-start(bf16[8,16,512]{2,1,0:T(8,128)(2,1)} %bitcast.1), calls=%async_computation.2 | async-start | bytes 262144 | tf_op jit(solution)/shard_map/all_to_all | solution.py:64
Sparse Core Ops, SparseCore 0:
  11.0 54.8 all-gather.3
Sparse Core Ops, SparseCore 1:
  53.4 34.3 reduce-scatter.4
  89.9 36.4 reduce-scatter.2
  131.1 34.1 all-gather.5
  167.6 31.9 all-gather.7
where the time goes:
time: 261 us; the launch traced here: 260 us
  waiting for transfers between devices  136 us (52%)
  blocking collectives  37.6 us (14%)
  matrix products  35.4 us (14%)
  starting transfers between devices  20.9 us (8%)
  between operations  15.7 us (6%)
  other arithmetic  8.13 us (3%)
  local copies, waits for them, and re-layouts  6.64 us (3%)
    all_gather x2, waiting for transfers between devices, hidden_panel(): return lax.all_gather(local_rows, 'col', axis=0, tiled=True)  55.2 us
    reduce_scatter x2, waiting for transfers between devices, width_split(): lax.psum_scatter(term.astype(jnp.bfloat16), 'col', scatter_dimension=0, t...  54.6 us
    all_to_all x1, blocking collectives, token_panel_a2a(): lax.all_to_all(copies, 'row', split_axis=0, concat_axis=0, tiled=True)  37.6 us
    all_gather x1, waiting for transfers between devices, token_panel(): return lax.all_gather(local_rows, 'row', axis=0, tiled=True)  12.5 us
    all_to_all x2, starting transfers between devices, unit_sum(): lax.all_to_all(pieces, 'row', split_axis=0, concat_axis=0, tiled=True)  12.1 us
    dot_general x2, matrix products, contract_last(): lax.dot_general(left, right, (((1,), (1,)), ((), ())), preferred_element_...  10.5 us
    all_to_all x2, waiting for transfers between devices, unit_sum(): lax.all_to_all(pieces, 'row', split_axis=0, concat_axis=0, tiled=True)  9.4 us
    all_to_all x1, starting transfers between devices, local(): lax.all_to_all(block_rows, 'col', split_axis=0, concat_axis=1, tiled=True)  8.57 us
  transfers between devices with their start and end apart: 8, of which 8 were waited for; matrix products, arithmetic and copies ran while one was open for 17% of the time, Pallas kernels for 0%

commit v1 on v0

--- a/solution.py
+++ b/solution.py
@@ -2,6 +2,7 @@
 import jax.numpy as jnp
 from jax import lax
 from jax.sharding import PartitionSpec as P
+from jax.lax import axis_index, axis_size, ppermute
 
 
 def gelu_grad(value):
@@ -61,7 +62,22 @@
     dpre_all = hidden_panel((dact_part * gelu_grad(pre_part)).astype(jnp.bfloat16))
     mixed = unit_sum(act_all, w_out, False)
     block_rows = (tokens.astype(jnp.float32) + mixed).astype(jnp.bfloat16)
-    block_out = lax.all_to_all(block_rows, "col", split_axis=0, concat_axis=1, tiled=True)
+    o_now = axis_size("col")
+    lower = axis_index("col")
+    y1, mat_out = (o_now, lower)
+    before = list(block_rows.shape)
+    val2 = block_rows.shape[0] // y1
+    before[0] = val2
+    reached = before[1]
+    before[1] = reached * y1
+    block_out = jnp.zeros(before, block_rows.dtype)
+    for i in [*range(y1)]:
+        high = lax.dynamic_slice_in_dim(block_rows, (mat_out ^ i) * val2, val2, axis=0)
+        if i:
+            high = ppermute(high, axis_name="col", perm=[(src_i, src_i ^ i) for src_i in range(y1)])
+        block_out = lax.dynamic_update_slice_in_dim(
+            block_out, high, (mat_out ^ i) * reached, axis=1
+        )
     grad_out = lax.dot_general(
         act_all, upstream_all, (((0,), (0,)), ((), ())), preferred_element_type=jnp.float32
     )

time: 261 us -> 266 us (1.019)
  starting transfers between devices: 20.9 us -> 26.7 us
    ppermute x0 -> x7, starting transfers between devices: none -> 14.4 us  [local(): ppermute(high, axis_name='col', perm=[(src_i, src_i ^ i) for src_i in ran...]
    all_to_all x1 -> x0, starting transfers between devices: 8.57 us -> none  [local(): lax.all_to_all(block_rows, 'col', split_axis=0, concat_axis=1, tiled=True)]
    ppermute x0 -> x7, waiting for transfers between devices: none -> 3.49 us  [local(): ppermute(high, axis_name='col', perm=[(src_i, src_i ^ i) for src_i in ran...]
    all_to_all x1 -> x0, waiting for transfers between devices: 2.68 us -> none  [local(): lax.all_to_all(block_rows, 'col', split_axis=0, concat_axis=1, tiled=True)]
    unnamed x11 -> x17, local copies, waits for them, and re-layouts: 4.88 us -> 6.87 us
  transfers between devices with their start and end apart: 8 -> 14, of which waited for: 8 -> 9; matrix products, arithmetic and copies ran while one was open for 17% -> 15% of each run, Pallas kernels for 0% -> 0%
where the time goes in v1:
time: 266 us; the launch traced here: 265 us
  waiting for transfers between devices  136 us (51%)
  blocking collectives  37.6 us (14%)
  matrix products  35.6 us (13%)
  starting transfers between devices  26.7 us (10%)
  between operations  15.9 us (6%)
  local copies, waits for them, and re-layouts  8.06 us (3%)
  other arithmetic  5.86 us (2%)
    all_gather x2, waiting for transfers between devices, hidden_panel(): return lax.all_gather(local_rows, 'col', axis=0, tiled=True)  55.2 us
    reduce_scatter x2, waiting for transfers between devices, width_split(): lax.psum_scatter(term.astype(jnp.bfloat16), 'col', scatter_dimension=0, t...  54.6 us
    all_to_all x1, blocking collectives, token_panel_a2a(): lax.all_to_all(copies, 'row', split_axis=0, concat_axis=0, tiled=True)  37.6 us
    ppermute x7, starting transfers between devices, local(): ppermute(high, axis_name='col', perm=[(src_i, src_i ^ i) for src_i in ran...  14.4 us
    all_gather x1, waiting for transfers between devices, token_panel(): return lax.all_gather(local_rows, 'row', axis=0, tiled=True)  12.5 us
    all_to_all x2, starting transfers between devices, unit_sum(): lax.all_to_all(pieces, 'row', split_axis=0, concat_axis=0, tiled=True)  12.1 us
    dot_general x2, matrix products, contract_last(): lax.dot_general(left, right, (((1,), (1,)), ((), ())), preferred_element_...  10.5 us
    all_to_all x2, waiting for transfers between devices, unit_sum(): lax.all_to_all(pieces, 'row', split_axis=0, concat_axis=0, tiled=True)  8.26 us
  transfers between devices with their start and end apart: 14, of which 9 were waited for; matrix products, arithmetic and copies ran while one was open for 15% of the time, Pallas kernels for 0%

profile of v1, /device:TPU:1, one launch (start us, length us, event | category | flops | bytes accessed | tf_op | source)
XLA Modules:
  0.0 265.2 jit_solution(11316369498597218609)
XLA Ops:
  9.9 37.6 %all_to_all.19 = bf16[16,128,512]{2,1,0:T(8,128)(2,1)S(1)} all-to-all(bf16[16,128,512]{2,1,0:T(8,128)(2,1)S(1)} %broadcast_in_dim.10), channel_id=1, replica_groups=mesh['row'=16,'col'=8] {'row'}, dimensions={0} | all-to-all | bytes 4194304 | tf_op jit(solution)/shard_map/all_to_all | solution.py:22
  47.5 1.4 copy-done.3
  48.9 4.3 %convolution_convert_fusion = bf16[2048,1024]{1,0:T(8,128)(2,1)} fusion(bf16[2048,512]{1,0:T(8,128)(2,1)S(1)} %bitcast.17, bf16[1024,512]{1,0:T(8,128)(2,1)S(1)} %copy-done), kind=kOutput, calls=%fused_computation.2 | convolution fusion | flops 2149580800 | bytes 7340032 | tf_op jit(solution)/shard_map/dot_general | solution.py:30
  53.3 12.5 %all-gather.4.cloned.1.call-done = bf16[2048,512]{1,0:T(8,128)(2,1)} async-done(((bf16[128,512]{1,0:T(8,128)(2,1)}), bf16[2048,512]{1,0:T(8,128)(2,1)}) %all-gather.4.cloned.1.call-update) | async-done | bytes 2097168 | tf_op jit(solution)/shard_map/all_gather | solution.py:15
  65.8 6.0 %convolution_convert_fusion.1 = bf16[2048,1024]{1,0:T(8,128)(2,1)} fusion(bf16[2048,512]{1,0:T(8,128)(2,1)} %all-gather.4.cloned.1.call-done, bf16[512,1024]{1,0:T(8,128)(2,1)S(1)} %copy-done.7), kind=kOutput, calls=%fused_computation.3 | convolution fusion | flops 2149580800 | bytes 7340032 | tf_op jit(solution)/shard_map/dot_general | solution.py:39
  71.9 15.8 %reduce-scatter.5.cloned.1.call-done = bf16[256,1024]{1,0:T(8,128)(2,1)} async-done(((bf16[2048,1024]{1,0:T(8,128)(2,1)}), bf16[256,1024]{1,0:T(8,128)(2,1)}) %reduce-scatter.5.cloned.1.call-update) | async-done | bytes 524304 | tf_op jit(solution)/shard_map/reduce_scatter | solution.py:40
  87.7 38.9 %reduce-scatter.3.cloned.1.call-done = bf16[256,1024]{1,0:T(8,128)(2,1)} async-done(((bf16[2048,1024]{1,0:T(8,128)(2,1)}), bf16[256,1024]{1,0:T(8,128)(2,1)}) %reduce-scatter.3.cloned.1.call-update) | async-done | bytes 524304 | tf_op jit(solution)/shard_map/reduce_scatter | solution.py:40
  126.5 4.6 %fusion.38 = (bf16[256,1024]{1,0:T(8,128)(2,1)}, bf16[256,1024]{1,0:T(8,128)(2,1)}) fusion(bf16[256,1024]{1,0:T(8,128)(2,1)} %reduce-scatter.3.cloned.1.call-done, bf16[256,1024]{1,0:T(8,128)(2,1)} %reduce-scatter.5.cloned.1.call-done), kind=kLoop, calls=%fused_computation.52 | loop fusion | flops 20185088 | bytes 2097152 | tf_op jit(solution)/shard_map/convert_element_type | solution.py:62
  131.9 33.5 %all-gather.6.cloned.1.call-done = bf16[2048,1024]{1,0:T(8,128)(2,1)} async-done(((bf16[256,1024]{1,0:T(8,128)(2,1)}), bf16[2048,1024]{1,0:T(8,128)(2,1)}) %all-gather.6.cloned.1.call-update) | async-done | bytes 4194320 | tf_op jit(solution)/shard_map/all_gather | solution.py:26
  165.4 5.9 %convolution_convert_fusion.3 = bf16[2048,512]{1,0:T(8,128)(2,1)} fusion(bf16[2048,1024]{1,0:T(8,128)(2,1)} %all-gather.6.cloned.1.call-done, bf16[1024,512]{1,0:T(8,128)(2,1)S(1)} %copy-done), kind=kOutput, calls=%fused_computation.5 | convolution fusion | flops 2148532224 | bytes 7340032 | tf_op jit(solution)/shard_map/dot_general | solution.py:50
  171.3 6.7 %all-to-all-start = ((bf16[16,128,512]{2,1,0:T(8,128)(2,1)}), bf16[16,128,512]{2,1,0:T(8,128)(2,1)S(1)}, u32[]{:S(2)}, u32[]{:S(2)}) async-start(bf16[16,128,512]{2,1,0:T(8,128)(2,1)} %bitcast.20), calls=%async_computation.1 | async-start | bytes 4194304 | tf_op jit(solution)/shard_map/all_to_all | solution.py:52
  178.0 21.7 %all-gather.8.cloned.1.call-done = bf16[2048,1024]{1,0:T(8,128)(2,1)} async-done(((bf16[256,1024]{1,0:T(8,128)(2,1)}), bf16[2048,1024]{1,0:T(8,128)(2,1)}) %all-gather.8.cloned.1.call-update) | async-done | bytes 4194320 | tf_op jit(solution)/shard_map/all_gather | solution.py:26
  199.6 6.2 %convolution_convert_fusion.2 = bf16[2048,512]{1,0:T(8,128)(2,1)} fusion(bf16[2048,1024]{1,0:T(8,128)(2,1)} %all-gather.8.cloned.1.call-done, bf16[512,1024]{1,0:T(8,128)(2,1)} %param.5), kind=kOutput, calls=%fused_computation.4 | convolution fusion | flops 2148532224 | bytes 7340032 | tf_op jit(solution)/shard_map/dot_general | solution.py:30
  208.5 5.4 %all-to-all-start.2 = ((bf16[16,128,512]{2,1,0:T(8,128)(2,1)}), bf16[16,128,512]{2,1,0:T(8,128)(2,1)S(1)}, u32[]{:S(2)}, u32[]{:S(2)}) async-start(bf16[16,128,512]{2,1,0:T(8,128)(2,1)} %bitcast.19), calls=%async_computation.4 | async-start | bytes 4194304 | tf_op jit(solution)/shard_map/all_to_all | solution.py:52
  213.9 6.5 %convolution_bitcast_fusion = f32[512,1024]{0,1:T(8,128)} fusion(bf16[2048,1024]{1,0:T(8,128)(2,1)} %all-gather.8.cloned.1.call-done, bf16[2048,512]{1,0:T(8,128)(2,1)} %all-gather.4.cloned.1.call-done), kind=kOutput, calls=%fused_computation.12 | convolution fusion | flops 2147483648 | bytes 8388608 | tf_op jit(solution)/shard_map/dot_general | solution.py:84
  220.5 2.9 %copy.8 = f32[512,1024]{1,0:T(8,128)} copy(f32[512,1024]{0,1:T(8,128)} %convolution_bitcast_fusion) | data formatting | bytes 4194304
  223.4 6.7 %fusion.39 = f32[1024,512]{1,0:T(8,128)} fusion(bf16[2048,1024]{1,0:T(8,128)(2,1)} %all-gather.6.cloned.1.call-done, bf16[2048,512]{1,0:T(8,128)(2,1)} %bitcast.18), kind=kOutput, calls=%fused_computation.70 | convolution fusion | flops 2147483648 | bytes 8388608 | tf_op jit(solution)/shard_map/dot_general | solution.py:81
  231.0 1.5 collective-permute-start
  232.5 6.9 %all-to-all-done.2 = bf16[16,128,512]{2,1,0:T(8,128)(2,1)S(1)} async-done(((bf16[16,128,512]{2,1,0:T(8,128)(2,1)}), bf16[16,128,512]{2,1,0:T(8,128)(2,1)S(1)}, u32[]{:S(2)}, u32[]{:S(2)}) %all-to-all-start.2) | async-done | bytes 2097184 | tf_op jit(solution)/shard_map/all_to_all | solution.py:52
  240.4 5.7 %collective-permute-start.6 = (bf16[16,512]{1,0:T(8,128)(2,1)S(1)}, bf16[16,512]{1,0:T(8,128)(2,1)S(1)}, u32[]{:S(2)}, u32[]{:S(2)}) collective-permute-start(bf16[16,512]{1,0:T(8,128)(2,1)S(1)} %get-tuple-element.10), channel_id=1, source_target_pairs={{0,7},{1,6},{2,5},{3,4},{4,3},{5,2},{6,1},{7,0},{8,15},{9,14},{10,... | collective-permute-start | bytes 49160 | tf_op jit(solution)/shard_map/ppermute | solution.py:77
  246.1 2.1 collective-permute-start.5
  250.0 2.1 collective-permute-done.1
  252.0 3.4 %collective-permute-start.2 = (bf16[16,512]{1,0:T(8,128)(2,1)S(1)}, bf16[16,512]{1,0:T(8,128)(2,1)S(1)}, u32[]{:S(2)}, u32[]{:S(2)}) collective-permute-start(bf16[16,512]{1,0:T(8,128)(2,1)S(1)} %get-tuple-element.14), channel_id=1, source_target_pairs={{0,3},{1,2},{2,1},{3,0},{4,7},{5,6},{6,5},{7,4},{8,11},{9,10},{10,... | collective-permute-start | bytes 49160 | tf_op jit(solution)/shard_map/ppermute | solution.py:77
  255.5 1.4 collective-permute-done.2
  (48 shorter events, 9.8 us)
Async XLA Ops:
  8.0 40.9 %copy-start = (bf16[1024,512]{1,0:T(8,128)(2,1)S(1)}, bf16[1024,512]{1,0:T(8,128)(2,1)}, u32[]{:S(2)}) copy-start(bf16[1024,512]{1,0:T(8,128)(2,1)} %param.6) | copy-start | bytes 3145732
  8.0 57.8 %all-gather.4.cloned.1.call-start = ((), (), s32[]{:S(2)}) async-start(), calls=%async_computation.5 | async-start | bytes 2228224 | tf_op jit(solution)/shard_map/all_gather | solution.py:15
  8.7 78.9 %reduce-scatter.5.cloned.1.call-start = ((), (), s32[]{:S(2)}) async-start(), calls=%async_computation.8 | async-start | bytes 4718592 | tf_op jit(solution)/shard_map/reduce_scatter | solution.py:40
  47.5 1.4 copy-start.3
  53.3 12.6 %copy-start.7 = (bf16[512,1024]{1,0:T(8,128)(2,1)S(1)}, bf16[512,1024]{1,0:T(8,128)(2,1)}, u32[]{:S(2)}) copy-start(bf16[512,1024]{1,0:T(8,128)(2,1)} %param.5) | copy-start | bytes 3145732
  53.3 73.2 %reduce-scatter.3.cloned.1.call-start = ((), (), s32[]{:S(2)}) async-start(), calls=%async_computation.6 | async-start | bytes 4718592 | tf_op jit(solution)/shard_map/reduce_scatter | solution.py:40
  71.8 93.6 %all-gather.6.cloned.1.call-start = ((), (), s32[]{:S(2)}) async-start(), calls=%async_computation.7 | async-start | bytes 4718592 | tf_op jit(solution)/shard_map/all_gather | solution.py:26
  131.1 68.5 %all-gather.8.cloned.1.call-start = ((), (), s32[]{:S(2)}) async-start(), calls=%async_computation.9 | async-start | bytes 4718592 | tf_op jit(solution)/shard_map/all_gather | solution.py:26
  171.3 35.9 %all-to-all-start = ((bf16[16,128,512]{2,1,0:T(8,128)(2,1)}), bf16[16,128,512]{2,1,0:T(8,128)(2,1)S(1)}, u32[]{:S(2)}, u32[]{:S(2)}) async-start(bf16[16,128,512]{2,1,0:T(8,128)(2,1)} %bitcast.20), calls=%async_computation.1 | async-start | bytes 4194304 | tf_op jit(solution)/shard_map/all_to_all | solution.py:52
  207.1 1.3 copy-start.1
  208.5 31.0 %all-to-all-start.2 = ((bf16[16,128,512]{2,1,0:T(8,128)(2,1)}), bf16[16,128,512]{2,1,0:T(8,128)(2,1)S(1)}, u32[]{:S(2)}, u32[]{:S(2)}) async-start(bf16[16,128,512]{2,1,0:T(8,128)(2,1)} %bitcast.19), calls=%async_computation.4 | async-start | bytes 4194304 | tf_op jit(solution)/shard_map/all_to_all | solution.py:52
  223.4 6.7 %copy-start.2 = (bf16[16,128,512]{2,1,0:T(8,128)(2,1)S(1)}, bf16[16,128,512]{2,1,0:T(8,128)(2,1)}, u32[]{:S(2)}) copy-start(bf16[16,128,512]{2,1,0:T(8,128)(2,1)} %copy-done.1) | copy-start | bytes 6291460
  230.0 0.9 copy-start.5
  230.9 8.8 %copy-start.4 = (bf16[128,512]{1,0:T(8,128)(2,1)S(1)}, bf16[128,512]{1,0:T(8,128)(2,1)}, u32[]{:S(2)}) copy-start(bf16[128,512]{1,0:T(8,128)(2,1)} %param.7) | copy-start | bytes 393220
  231.0 18.4 %collective-permute-start = (bf16[16,512]{1,0:T(8,128)(2,1)S(1)}, bf16[16,512]{1,0:T(8,128)(2,1)S(1)}, u32[]{:S(2)}, u32[]{:S(2)}) collective-permute-start(bf16[16,512]{1,0:T(8,128)(2,1)S(1)} %get-tuple-element.16), channel_id=1, source_target_pairs={{0,1},{1,0},{2,3},{3,2},{4,5},{5,4},{6,7},{7,6},{8,9},{9,8},{10,11... | collective-permute-start | bytes 49160 | tf_op jit(solution)/shard_map/ppermute | solution.py:77
  240.4 16.5 %collective-permute-start.6 = (bf16[16,512]{1,0:T(8,128)(2,1)S(1)}, bf16[16,512]{1,0:T(8,128)(2,1)S(1)}, u32[]{:S(2)}, u32[]{:S(2)}) collective-permute-start(bf16[16,512]{1,0:T(8,128)(2,1)S(1)} %get-tuple-element.10), channel_id=1, source_target_pairs={{0,7},{1,6},{2,5},{3,4},{4,3},{5,2},{6,1},{7,0},{8,15},{9,14},{10,... | collective-permute-start | bytes 49160 | tf_op jit(solution)/shard_map/ppermute | solution.py:77
  246.1 10.8 %collective-permute-start.5 = (bf16[16,512]{1,0:T(8,128)(2,1)S(1)}, bf16[16,512]{1,0:T(8,128)(2,1)S(1)}, u32[]{:S(2)}, u32[]{:S(2)}) collective-permute-start(bf16[16,512]{1,0:T(8,128)(2,1)S(1)} %get-tuple-element.11), channel_id=1, source_target_pairs={{0,6},{1,7},{2,4},{3,5},{4,2},{5,3},{6,0},{7,1},{8,14},{9,15},{10,... | collective-permute-start | bytes 49160 | tf_op jit(solution)/shard_map/ppermute | solution.py:77
  248.3 8.6 %collective-permute-start.4 = (bf16[16,512]{1,0:T(8,128)(2,1)S(1)}, bf16[16,512]{1,0:T(8,128)(2,1)S(1)}, u32[]{:S(2)}, u32[]{:S(2)}) collective-permute-start(bf16[16,512]{1,0:T(8,128)(2,1)S(1)} %get-tuple-element.12), channel_id=1, source_target_pairs={{0,5},{1,4},{2,7},{3,6},{4,1},{5,0},{6,3},{7,2},{8,13},{9,12},{10,... | collective-permute-start | bytes 49160 | tf_op jit(solution)/shard_map/ppermute | solution.py:77
  248.3 8.6 %collective-permute-start.3 = (bf16[16,512]{1,0:T(8,128)(2,1)S(1)}, bf16[16,512]{1,0:T(8,128)(2,1)S(1)}, u32[]{:S(2)}, u32[]{:S(2)}) collective-permute-start(bf16[16,512]{1,0:T(8,128)(2,1)S(1)} %get-tuple-element.13), channel_id=1, source_target_pairs={{0,4},{1,5},{2,6},{3,7},{4,0},{5,1},{6,2},{7,3},{8,12},{9,13},{10,... | collective-permute-start | bytes 49160 | tf_op jit(solution)/shard_map/ppermute | solution.py:77
  249.4 2.6 collective-permute-start.1
  252.0 4.8 %collective-permute-start.2 = (bf16[16,512]{1,0:T(8,128)(2,1)S(1)}, bf16[16,512]{1,0:T(8,128)(2,1)S(1)}, u32[]{:S(2)}, u32[]{:S(2)}) collective-permute-start(bf16[16,512]{1,0:T(8,128)(2,1)S(1)} %get-tuple-element.14), channel_id=1, source_target_pairs={{0,3},{1,2},{2,1},{3,0},{4,7},{5,6},{6,5},{7,4},{8,11},{9,10},{10,... | collective-permute-start | bytes 49160 | tf_op jit(solution)/shard_map/ppermute | solution.py:77
  257.0 0.7 copy-start.6
Sparse Core Ops, SparseCore 0:
  11.0 54.8 all-gather.3
Sparse Core Ops, SparseCore 1:
  53.4 34.3 reduce-scatter.4
  90.0 36.5 reduce-scatter.2
  131.2 34.1 all-gather.5
  167.7 31.9 all-gather.7
